TPU v7x, 32 devices: a whole 2x2x4 slice. The times are simulated.
32 devices in a mesh: pat: 8 (over y, x, core), feat: 4 (over z).
Axes of the slice: x: 2, y: 2, z: 4, core: 2. Of those that a mesh axis runs over, the one named last changes fastest.
Arguments:
- visits: bfloat16 [32768, 8192], P('pat', 'feat'), may hold values from -1.5 to 1.5
- counts: int32 [64], P('pat'), may hold values from 128 to 512, as said below
- patient_weight: float32 [64, 128], P('pat'), may hold values from 0.5 to 2
- phenotype_core: float32 [128, 128], replicated, may hold values from -0.5 to 0.5
- feature_factor: bfloat16 [8192, 128], P('feat'), may hold values from -0.0625 to 0.0625
- static_data: bfloat16 [64, 4096], P('pat', 'feat'), may hold values from -6 to 6
- static_factor: bfloat16 [4096, 128], P('feat'), may hold values from -0.09375 to 0.09375
Outputs:
- core_new: float32 [128, 128], replicated
- feature_new: float32 [8192, 128], P('feat')
- patient_new: float32 [64, 128], P('pat')
- static_new: float32 [4096, 128], P('feat')
Inputs may be any that keep to these rules, and one draw needn't show every extreme that they name: `counts`: some patient of the last index of pat has exactly 512 visits.
All inputs are finite; a program needn't handle non-finite values.
Results may differ from a plain program's by a relative error of at most 0.0035.
Values may be sent and summed in bfloat16 or wider, within the bound.
A program may use at most 64 MiB of HBM per device.

v0:
```python
import jax
import jax.numpy as jnp
from jax import lax
from jax.sharding import PartitionSpec as P

BLK = 128
SUB = 32
NS_STEPS = 8


MU_RIDGE = 1.0


def layout(counts, rows):
    padded = (counts + BLK - 1) // BLK * BLK
    starts = jnp.cumsum(padded) - padded
    positions = jnp.arange(rows, dtype=jnp.int32)
    live = (positions[:, None] >= starts[None, :]) & (
        positions[:, None] < (starts + counts)[None, :]
    )
    leading = positions[::SUB]
    member = (leading[:, None] >= starts[None, :]) & (leading[:, None] < (starts + padded)[None, :])
    return (live.astype(jnp.float32), member.astype(jnp.float32))


def contract_rows(left, right):
    return lax.dot_general(left, right, (((0,), (0,)), ((), ())), precision=lax.Precision.HIGHEST)


def narrow_rows(left, right):
    return lax.dot_general(
        left, right, (((0,), (0,)), ((), ())), preferred_element_type=jnp.float32
    )


def core_field(projected, weight_rows, core):
    return lax.dot_general(
        projected * weight_rows, core, (((1,), (1,)), ((), ())), precision=lax.Precision.HIGHEST
    )


def block_grams(field, block_owner):
    pieces = field.reshape(-1, SUB, field.shape[1])
    grams = jnp.einsum("bvr,bvs->brs", pieces, pieces, precision=lax.Precision.HIGHEST)
    return jnp.einsum("bp,brs->prs", block_owner, grams, precision=lax.Precision.HIGHEST)


def batched(left, right):
    return jnp.einsum("nij,njk->nik", left, right, precision=lax.Precision.HIGHEST)


def polar_factor(grams):
    identity = jnp.eye(grams.shape[-1], dtype=jnp.float32)
    traces = jnp.trace(grams, axis1=1, axis2=2)
    moment = grams / traces[:, None, None]
    factor = identity[None] / jnp.sqrt(traces)[:, None, None]
    for iteration in range(NS_STEPS):
        correction = 1.5 * identity - 0.5 * moment
        factor = batched(factor, correction)
        moment = batched(batched(correction, moment), correction)
    return factor


def finish(field, projected, weight_rows, block_owner, row_owner, factor, core):
    rank = field.shape[1]
    block_factor = jnp.einsum("bp,prs->brs", block_owner, factor, precision=lax.Precision.HIGHEST)
    pieces = field.reshape(-1, SUB, rank)
    ortho = jnp.einsum(
        "bvr,brs->bvs", pieces, block_factor, precision=lax.Precision.HIGHEST
    ).reshape(-1, rank)
    mapped = jnp.dot(ortho, core, precision=lax.Precision.HIGHEST)
    patient_terms = contract_rows(row_owner, mapped * projected)
    core_terms = contract_rows(ortho, projected * weight_rows)
    update = (mapped * weight_rows).astype(jnp.bfloat16)
    return (patient_terms, core_terms, update)


def solve_right(rhs, matrix):
    lower = jnp.linalg.cholesky(matrix)
    return jax.scipy.linalg.cho_solve((lower, True), rhs.T).T


def local(
    visits, counts, patient_weight, phenotype_core, feature_factor, static_data, static_factor
):
    rank = phenotype_core.shape[0]
    identity = jnp.eye(rank, dtype=jnp.float32)
    core_gram = contract_rows(phenotype_core, phenotype_core)
    weight_gram_part = contract_rows(patient_weight, patient_weight)
    feature_gram_part = narrow_rows(feature_factor, feature_factor)
    static_gram_part = narrow_rows(static_factor, static_factor)
    coupled_part = jnp.dot(static_data, static_factor, preferred_element_type=jnp.float32)
    static_terms_part = contract_rows(static_data.astype(jnp.float32), patient_weight)
    projected_part = jnp.dot(visits, feature_factor, preferred_element_type=jnp.float32)
    rows_all = visits.shape[0]
    projected, coupled, feature_gram, static_gram = lax.psum(
        (projected_part, coupled_part, feature_gram_part, static_gram_part), "feat"
    )
    row_owner, block_owner = layout(counts, rows_all)
    weight_rows = jnp.dot(row_owner, patient_weight, precision=lax.Precision.HIGHEST)
    field = core_field(projected, weight_rows, phenotype_core)
    factor = polar_factor(block_grams(field, block_owner))
    patient_terms, core_terms_part, update = finish(
        field, projected, weight_rows, block_owner, row_owner, factor, phenotype_core
    )
    feature_terms_part = narrow_rows(visits, update)
    feature_terms, core_terms, static_terms, weight_gram = lax.psum(
        (feature_terms_part, core_terms_part, static_terms_part, weight_gram_part), "pat"
    )
    feature_new = solve_right(feature_terms, core_gram * weight_gram + MU_RIDGE * identity)
    core_new = solve_right(core_terms, feature_gram * weight_gram + MU_RIDGE * identity)
    patient_new = solve_right(
        patient_terms + coupled, core_gram * feature_gram + static_gram + MU_RIDGE * identity
    )
    static_new = solve_right(static_terms, weight_gram + MU_RIDGE * identity)
    return (core_new, feature_new, patient_new, static_new)


def solution(mesh):
    return jax.shard_map(
        local,
        mesh=mesh,
        in_specs=(
            P("pat", "feat"),
            P("pat"),
            P("pat", None),
            P(),
            P("feat", None),
            P("pat", "feat"),
            P("feat", None),
        ),
        out_specs=(P(), P("feat", None), P("pat", None), P("feat", None)),
        check_vma=False,
    )
```

profile of v0, /device:TPU:0, one launch (start us, length us, event | category | flops | bytes accessed | tf_op | source)
XLA Modules:
  0.0 353.5 jit_solution(7302844279100633003)
XLA Ops:
  7.2 1.0 copy-done
  8.2 1.0 fusion.111
  9.2 9.5 %fusion.113 = f32[4096,128]{1,0:T(8,128)} fusion(bf16[4096,2048]{1,0:T(8,128)(2,1)} %param.8, bf16[2048,128]{1,0:T(8,128)(2,1)S(1)} %copy-done), kind=kOutput, calls=%fused_computation.151 | convolution fusion | flops 2147483648 | bytes 19398656 | tf_op jit(solution)/shard_map/dot_general | solution.py:94
  21.3 1.2 fusion.120
  22.6 90.3 %all-reduce.7.cloned.1.call-done = (f32[4096,128]{1,0:T(8,128)}, f32[128,128]{1,0:T(8,128)}, f32[128,128]{1,0:T(8,128)}) async-done(((f32[4096,128]{1,0:T(8,128)}, f32[128,128]{1,0:T(8,128)}, f32[128,128]{1,0:T(8,128)}), (f32[4096,128]{1,0:T(8,128)}, f32[128,128]{1,0:T(8,128)}, f32[128,128]{1,0:T(8,128)})) %all-reduce.7.cloned.1.call-update) | async-done | bytes 2228240 | tf_op jit(solution)/shard_map/psum | solution.py:96
  112.9 3.5 fusion.110
  116.4 1.8 fusion.114
  118.2 13.8 %fusion.115 = f32[128,128,128]{2,1,0:T(8,128)S(1)} fusion(f32[128,32,128]{2,1,0:T(8,128)S(1)} %bitcast.115), kind=kOutput, calls=%fused_computation.153 | convolution fusion | flops 805306368 | bytes 10485760 | tf_op jit(solution)/shard_map/bvr,bvs->brs/dot_general | solution.py:44
  132.0 7.8 %select_reduce_fusion = (f32[8]{0:T(128)S(1)}, f32[8,128,128]{2,0,1:T(8,128)S(1)}) fusion(pred[128,128]{1,0:T(8,128)(4,1)S(1)} %iota_compare_fusion.2, f32[128,128,128]{2,1,0:T(8,128)S(1)} %fusion.115, s32[128]{0:T(128)S(1)} %slice.57, s32[8]{0:T(128)S(1)} %bitcast.119, s32[8]{0:T(128)S(1)} %get-tuple-element.15), kind=kOutput, calls=%fused_computation.32 | convolution fusion | flops 201591808 | bytes 8929888 | tf_op jit(solution)/shard_map/bp,brs->prs/dot_general | solution.py:45
  149.4 0.9 fusion.34
  158.0 3.5 %fusion.11 = f32[128,128,128]{2,0,1:T(8,128)S(1)} fusion(f32[8,128,128]{2,1,0:T(8,128)S(1)} %fusion.13, s32[128]{0:T(128)S(1)} %slice.57, s32[8]{0:T(128)S(1)} %bitcast.120, s32[8]{0:T(128)S(1)} %get-tuple-element.15), kind=kOutput, calls=%fused_computation.11 | convolution fusion | flops 201329664 | bytes 8913472 | tf_op jit(solution)/shard_map/bp,prs->brs/dot_general | solution.py:66
  161.5 11.9 %fusion = f32[128,32,128]{2,1,0:T(8,128)S(1)} fusion(f32[128,32,128]{2,1,0:T(8,128)S(1)} %bitcast.116, f32[128,128,128]{2,0,1:T(8,128)S(1)} %fusion.11), kind=kOutput, calls=%fused_computation | convolution fusion | flops 805306368 | bytes 12582912 | tf_op jit(solution)/shard_map/bvr,brs->bvs/dot_general | solution.py:68
  173.4 2.0 fusion.117
  175.4 4.1 %fusion.116 = f32[128,128]{1,0:T(8,128)} fusion(f32[4096,128]{1,0:T(8,128)S(1)} %bitcast.118, f32[4096,128]{1,0:T(8,128)S(1)} %get-tuple-element.20), kind=kOutput, calls=%fused_computation.154 | convolution fusion | flops 805306368 | bytes 4259840 | tf_op jit(solution)/shard_map/dot_general | solution.py:27
  179.5 3.4 convolution_bitcast_fusion
  183.1 10.1 %psum.62 = f32[8,128]{1,0:T(8,128)S(1)} all-reduce(f32[8,128]{1,0:T(8,128)S(1)} %fusion.119), channel_id=1, replica_groups=mesh['pat'=8,'feat'=4] {'feat'}, use_global_device_ids=true, to_apply=%region_10.12 | all-reduce | flops 1024 | bytes 8192 | tf_op jit(solution)/shard_map/psum | solution.py:96
  193.3 2.5 fusion.6
  195.8 46.1 %all-reduce.5.cloned.1.call-done = (f32[128,128]{1,0:T(8,128)}, f32[128,128]{1,0:T(8,128)}, f32[2048,128]{0,1:T(8,128)}, f32[1024,128]{1,0:T(8,128)}) async-done(((f32[128,128]{1,0:T(8,128)}, f32[128,128]{1,0:T(8,128)}, f32[2048,128]{0,1:T(8,128)}, f32[1024,128]{1,0:T(8,128)}), (f32[128,128]{1,0:T(8,128)}, f32[128,128]{1,0:T(8,128)}, f32[2048,128]{0,1:T(8,128)}, ...) | async-done | bytes 1703952 | tf_op jit(solution)/shard_map/psum | solution.py:107
  241.9 1.1 convert_add_fusion
  244.1 11.7 %cholesky.107 = f32[128,128]{1,0:T(8,128)S(1)} custom-call(f32[128,128]{1,0:T(8,128)S(1)} %copy.50), custom_call_target="Cholesky" | custom-call | tf_op jit(solution)/shard_map/jit(cholesky)/cholesky | solution.py:79
  257.2 9.8 %custom-call.33 = f32[1,128,128]{1,2,0:T(8,128)S(1)} custom-call(f32[1,128,128]{2,1,0:T(8,128)S(1)} %fusion.73), custom_call_target="InvertDiagBlocksLowerTriangular" | custom-call | tf_op jit(solution)/shard_map/jit(_cho_solve)/triangular_solve | solution.py:80
  267.0 1.7 fusion.76
  268.7 1.8 fusion.74
  270.8 12.1 %cholesky.96 = f32[128,128]{1,0:T(8,128)S(1)} custom-call(f32[128,128]{1,0:T(8,128)S(1)} %copy.48), custom_call_target="Cholesky" | custom-call | tf_op jit(solution)/shard_map/jit(cholesky)/cholesky | solution.py:79
  284.2 9.8 %custom-call.32 = f32[1,128,128]{1,2,0:T(8,128)S(1)} custom-call(f32[1,128,128]{2,1,0:T(8,128)S(1)} %fusion.72), custom_call_target="InvertDiagBlocksLowerTriangular" | custom-call | tf_op jit(solution)/shard_map/jit(_cho_solve)/triangular_solve | solution.py:80
  295.3 11.7 %cholesky.85 = f32[128,128]{1,0:T(8,128)S(1)} custom-call(f32[128,128]{1,0:T(8,128)S(1)} %copy.46), custom_call_target="Cholesky" | custom-call | tf_op jit(solution)/shard_map/jit(cholesky)/cholesky | solution.py:79
  308.4 9.8 %custom-call.31 = f32[1,128,128]{1,2,0:T(8,128)S(1)} custom-call(f32[1,128,128]{2,1,0:T(8,128)S(1)} %fusion.71), custom_call_target="InvertDiagBlocksLowerTriangular" | custom-call | tf_op jit(solution)/shard_map/jit(_cho_solve)/triangular_solve | solution.py:80
  318.2 1.1 fusion.86
  319.3 2.8 fusion.84
  322.2 11.9 %cholesky.74 = f32[128,128]{1,0:T(8,128)S(1)} custom-call(f32[128,128]{1,0:T(8,128)S(1)} %copy.32), custom_call_target="Cholesky" | custom-call | tf_op jit(solution)/shard_map/jit(cholesky)/cholesky | solution.py:79
  335.5 9.8 %custom-call.30 = f32[1,128,128]{1,2,0:T(8,128)S(1)} custom-call(f32[1,128,128]{2,1,0:T(8,128)S(1)} %fusion.70), custom_call_target="InvertDiagBlocksLowerTriangular" | custom-call | tf_op jit(solution)/shard_map/jit(_cho_solve)/triangular_solve | solution.py:80
  345.6 0.9 fusion.89
  (101 shorter events, 28.2 us)
Async XLA Ops:
  7.2 1.1 copy-start
  7.2 105.7 %all-reduce.7.cloned.1.call-start = ((), (), s32[]{:S(2)}) async-start(), calls=%async_computation.1 | async-start | bytes 4456448 | tf_op jit(solution)/shard_map/psum | solution.py:96
  9.2 9.5 %copy-start.2 = (bf16[1024,128]{1,0:T(8,128)(2,1)S(1)}, bf16[1024,128]{1,0:T(8,128)(2,1)}, u32[]{:S(2)}) copy-start(bf16[1024,128]{1,0:T(8,128)(2,1)} %param.14) | copy-start | bytes 786436
  18.6 1.5 copy-start.10
  18.6 1.8 copy-start.5
  18.6 2.7 copy-start.9
  19.6 222.3 %all-reduce.5.cloned.1.call-start = ((), (), s32[]{:S(2)}) async-start(), calls=%async_computation | async-start | bytes 3407872 | tf_op jit(solution)/shard_map/psum | solution.py:107
  112.9 3.5 copy-start.3
  157.2 22.3 %slice-start = ((s8[16777216]{0:T(1024)(128)(4,1)}), s8[4194304]{0:T(1024)(128)(4,1)S(1)}, s32[]{:S(2)}) async-start(s8[16777216]{0:T(1024)(128)(4,1)} %bitcast.113), calls=%async_computation.2 | async-start | bytes 8388608
  157.9 21.6 %slice-start.1 = ((s8[16777216]{0:T(1024)(128)(4,1)}), s8[4194304]{0:T(1024)(128)(4,1)S(1)}, s32[]{:S(2)}) async-start(s8[16777216]{0:T(1024)(128)(4,1)} %bitcast.113), calls=%async_computation.3 | async-start | bytes 8388608
  161.5 18.0 %slice-start.2 = ((s8[16777216]{0:T(1024)(128)(4,1)}), s8[4194304]{0:T(1024)(128)(4,1)S(1)}, s32[]{:S(2)}) async-start(s8[16777216]{0:T(1024)(128)(4,1)} %bitcast.113), calls=%async_computation.4 | async-start | bytes 8388608
  173.4 6.1 %slice-start.3 = ((s8[16777216]{0:T(1024)(128)(4,1)}), s8[4194304]{0:T(1024)(128)(4,1)S(1)}, s32[]{:S(2)}) async-start(s8[16777216]{0:T(1024)(128)(4,1)} %bitcast.113), calls=%async_computation.5 | async-start | bytes 8388608
  193.3 48.6 %copy-start.6 = (f32[128,128]{1,0:T(8,128)S(1)}, f32[128,128]{1,0:T(8,128)}, u32[]{:S(2)}) copy-start(f32[128,128]{1,0:T(8,128)} %get-tuple-element.10) | copy-start | bytes 196612
  193.3 48.6 %copy-start.7 = (f32[128,128]{1,0:T(8,128)S(1)}, f32[128,128]{1,0:T(8,128)}, u32[]{:S(2)}) copy-start(f32[128,128]{1,0:T(8,128)} %get-tuple-element.11) | copy-start | bytes 196612
  244.0 74.2 %copy-start.4 = (f32[2048,128]{0,1:T(8,128)S(1)}, f32[2048,128]{0,1:T(8,128)}, u32[]{:S(2)}) copy-start(f32[2048,128]{0,1:T(8,128)} %get-tuple-element.7) | copy-start | bytes 3145732
  318.2 27.1 %copy-start.8 = (f32[128,128]{1,0:T(8,128)S(1)}, f32[128,128]{1,0:T(8,128)}, u32[]{:S(2)}) copy-start(f32[128,128]{1,0:T(8,128)} %get-tuple-element.5) | copy-start | bytes 196612
  318.2 28.3 %copy-start.1 = (bf16[2048,128]{1,0:T(8,128)(2,1)S(1)}, bf16[2048,128]{1,0:T(8,128)(2,1)}, u32[]{:S(2)}) copy-start(bf16[2048,128]{1,0:T(8,128)(2,1)} %param.12) | copy-start | bytes 1572868
Sparse Core Ops, SparseCore 0:
  19.7 93.1 all-reduce.6
  183.1 58.7 all-reduce.4
where the time goes:
time: 357 us; the launch traced here: 354 us
  waiting for transfers between devices  136 us (38%)
  other arithmetic  95.6 us (27%)
  matrix products  94.2 us (26%)
  between operations  14.9 us (4%)
  blocking collectives  10.1 us (3%)
    psum x1, waiting for transfers between devices, local(): lax.psum((projected_part, coupled_part, feature_gram_part, static_gram_pa...  90.3 us
    another operation x13, other arithmetic, solve_right(): lower = jnp.linalg.cholesky(matrix)  50.1 us
    psum x1, waiting for transfers between devices, local(): lax.psum((feature_terms_part, core_terms_part, static_terms_part, weight_...  46.1 us
    another operation x8, other arithmetic, solve_right(): return jax.scipy.linalg.cho_solve((lower, True), rhs.T).T  41.9 us
    dot_general x22, matrix products, batched(): jnp.einsum('nij,njk->nik', left, right, precision=lax.Precision.HIGHEST)  15.5 us
    dot_general x1, matrix products, block_grams(): jnp.einsum('bvr,bvs->brs', pieces, pieces, precision=lax.Precision.HIGHEST)  13.8 us
    dot_general x1, matrix products, finish(): jnp.einsum('bvr,brs->bvs', pieces, block_factor, precision=lax.Precision....  11.9 us
    psum x1, blocking collectives, local(): lax.psum((projected_part, coupled_part, feature_gram_part, static_gram_pa...  10.1 us
  transfers between devices with their start and end apart: 2, of which 2 were waited for; matrix products, arithmetic and copies ran while one was open for 1% of the time, Pallas kernels for 0%

commit v1 on v0

v1 whole, which is shorter than its diff:
```python
import functools

import jax
import jax.numpy as jnp
from jax import lax
from jax.experimental import pallas as pl
from jax.experimental.pallas import tpu as pltpu
from jax.sharding import PartitionSpec as P

BLK = 128
NS_STEPS = 8
MU_RIDGE = 1.0
F32 = jnp.float32
BF16 = jnp.bfloat16
MESH = pl.DeviceIdType.MESH

NN = (((1,), (0,)), ((), ()))
NT = (((1,), (1,)), ((), ()))
TN = (((0,), (0,)), ((), ()))


def dg(a, b, dims):
    return lax.dot_general(a, b, dims, preferred_element_type=F32)


def split(x):
    hi = x.astype(BF16)
    return hi, (x - hi.astype(F32)).astype(BF16)


def dot3(a, b, dims=NN):
    a_hi, a_lo = split(a)
    b_hi, b_lo = split(b)
    return dg(a_hi, b_hi, dims) + (dg(a_hi, b_lo, dims) + dg(a_lo, b_hi, dims))


def exact(a, b, dims=NN):
    return lax.dot_general(
        a, b, dims, precision=lax.Precision.HIGHEST, preferred_element_type=F32
    )


def solve(rhs, matrix, inverse):
    guess = dot3(rhs, inverse)
    return guess + dot3(rhs - exact(guess, matrix), inverse)


def kernel(
    n_pat, n_feat, chunks, tiles,
    counts, visits, weight, core, factor_in, static_data, static_factor,
    core_new, feature_new, patient_new, static_new,
    vis, proj, part, low_in, high_in, total,
    gram_out, gram_low, gram_high, gram_total, weights_all, static_all,
    mats, inverses, wides, row_weights, squares, grams, factors, halves, updates,
    terms_out, terms_in, core_out, core_in, new_out, new_in, coreg_out, coreg_in,
    vis_sem, part_send, low_recv, high_recv, total_send, total_recv,
    gram_sem, weight_send, weight_recv, static_send, static_recv,
    terms_send, terms_recv, core_send, core_recv,
    new_send, new_recv, coreg_send, coreg_recv,
):
    me = lax.axis_index("pat")
    z = lax.axis_index("feat")
    rank = core.shape[0]
    rows = visits.shape[0]
    rows_chunk = rows // chunks
    patients = weight.shape[0]
    features = visits.shape[1]
    piece = features // n_pat
    owners, core_rows = core_out.shape[0], core_out.shape[1]
    inner = z > 0
    outer = z < n_feat - 1

    def remote(src, dst, send, recv, **where):
        return pltpu.make_async_remote_copy(
            src_ref=src, dst_ref=dst, send_sem=send, recv_sem=recv,
            device_id=where, device_id_type=MESH,
        )

    def span(c):
        return pl.ds(pl.multiple_of(c * rows_chunk, rows_chunk), rows_chunk)

    def load(c):
        return pltpu.make_async_copy(visits.at[span(c)], vis.at[span(c)], vis_sem.at[c])

    @pl.loop(0, chunks)
    def _(c):
        load(c).start()

    barrier = pltpu.get_barrier_semaphore()
    for d in range(1, n_pat):
        pl.semaphore_signal(
            barrier, inc=1, device_id={"pat": lax.rem(me + d, n_pat)}, device_id_type=MESH
        )

    @pl.when(inner)
    def _():
        pl.semaphore_signal(barrier, inc=1, device_id={"feat": z - 1}, device_id_type=MESH)

    @pl.when(outer)
    def _():
        pl.semaphore_signal(barrier, inc=1, device_id={"feat": z + 1}, device_id_type=MESH)

    weights_all[me] = weight[...]
    static_all[me] = static_data[...].astype(F32)
    gram_own = jnp.concatenate(
        [
            dg(factor_in[...], factor_in[...], TN),
            dg(static_factor[...], static_factor[...], TN),
            dg(static_data[...], static_factor[...], NN),
        ],
        axis=0,
    )
    gram_out[...] = gram_own

    pl.semaphore_wait(
        barrier, n_pat - 1 + jnp.where(inner, 1, 0) + jnp.where(outer, 1, 0)
    )

    def gram_part(up):
        if up:
            return remote(gram_out, gram_low, gram_sem.at[0], gram_sem.at[1], feat=z + 1)
        return remote(gram_out, gram_high, gram_sem.at[0], gram_sem.at[2], feat=z - 1)

    def gram_back(up):
        return remote(
            gram_total, gram_total, gram_sem.at[4 if up else 3], gram_sem.at[5],
            feat=z + 1 if up else z - 1,
        )

    gram_owner = n_feat // 2

    @pl.when(z == 0)
    def _():
        gram_part(True).start()

    @pl.when(z == n_feat - 1)
    def _():
        gram_part(False).start()

    def weight_copy(d):
        peer = lax.rem(me + d, n_pat)
        return remote(
            weights_all.at[me], weights_all.at[me], weight_send.at[d], weight_recv.at[me], pat=peer
        )

    def static_copy(d):
        peer = lax.rem(me + d, n_pat)
        return remote(
            static_all.at[me], static_all.at[me], static_send.at[d], static_recv.at[me], pat=peer
        )

    for d in range(1, n_pat):
        weight_copy(d).start()
        static_copy(d).start()

    def owner_of(c):
        return n_feat // 2 - 1 + lax.rem(c, 2)

    def part_copy(c, up):
        if up:
            return remote(
                part.at[span(c)], low_in.at[span(c)], part_send.at[c], low_recv.at[c], feat=z + 1
            )
        return remote(
            part.at[span(c)], high_in.at[span(c)], part_send.at[c], high_recv.at[c], feat=z - 1
        )

    def total_copy(c, up):
        return remote(
            total.at[span(c)], total.at[span(c)], total_send.at[1 if up else 0, c],
            total_recv.at[c], feat=z + 1 if up else z - 1,
        )

    @pl.loop(0, chunks)
    def _(c):
        load(c).wait()
        product = dg(vis[span(c), :], factor_in[...], NN)
        proj[span(c), :] = product

        @pl.when(z == 0)
        def _():
            part[span(c), :] = product
            part_copy(c, True).start()

        @pl.when(z == n_feat - 1)
        def _():
            part[span(c), :] = product
            part_copy(c, False).start()

    @pl.when(inner & (z < gram_owner))
    def _():
        gram_part(True).wait_recv()
        gram_out[...] += gram_low[...]
        gram_part(True).start()

    @pl.when(outer & (z > gram_owner))
    def _():
        gram_part(False).wait_recv()
        gram_out[...] += gram_high[...]
        gram_part(False).start()

    @pl.when(z == gram_owner)
    def _():
        gram_part(True).wait_recv()
        gram_part(False).wait_recv()
        gram_total[...] = gram_out[...] + gram_low[...] + gram_high[...]
        gram_back(False).start()
        gram_back(True).start()

    def relay(c):
        owner = owner_of(c)

        @pl.when(inner & (z < owner))
        def _():
            part_copy(c, True).wait_recv()
            part[span(c), :] = proj[span(c), :] + low_in[span(c), :]
            part_copy(c, True).start()

        @pl.when(outer & (z > owner))
        def _():
            part_copy(c, False).wait_recv()
            part[span(c), :] = proj[span(c), :] + high_in[span(c), :]
            part_copy(c, False).start()

        @pl.when(z == owner)
        def _():
            part_copy(c, True).wait_recv()
            part_copy(c, False).wait_recv()
            total[span(c), :] = proj[span(c), :] + low_in[span(c), :] + high_in[span(c), :]
            total_copy(c, False).start()
            total_copy(c, True).start()

    def spread(c):
        owner = owner_of(c)

        @pl.when(z < owner)
        def _():
            total_copy(c, False).wait_recv()

            @pl.when(inner)
            def _():
                total_copy(c, False).start()

        @pl.when(z > owner)
        def _():
            total_copy(c, True).wait_recv()

            @pl.when(outer)
            def _():
                total_copy(c, True).start()

    lag = 4

    @pl.loop(0, lag)
    def _(c):
        relay(c)

    @pl.when(z < gram_owner)
    def _():
        gram_back(False).wait_recv()

        @pl.when(inner)
        def _():
            gram_back(False).start()

    @pl.when(z > gram_owner)
    def _():
        gram_back(True).wait_recv()

        @pl.when(outer)
        def _():
            gram_back(True).start()

    for d in range(1, n_pat):
        peer = lax.rem(me + d, n_pat)
        remote(
            weights_all.at[peer], weights_all.at[peer], weight_send.at[d], weight_recv.at[peer],
            pat=peer,
        ).wait_recv()
        remote(
            static_all.at[peer], static_all.at[peer], static_send.at[d], static_recv.at[peer],
            pat=peer,
        ).wait_recv()

    lane = lax.broadcasted_iota(jnp.int32, (rank, rank), 1)
    sub = lax.broadcasted_iota(jnp.int32, (rank, rank), 0)
    identity = (lane == sub).astype(F32)
    all_rows = weights_all[...].reshape(n_pat * patients, rank)
    weight_gram = exact(all_rows, all_rows, TN)
    core_gram = exact(core[...], core[...], TN)
    feature_gram = gram_total[pl.ds(0, rank), :]
    static_gram = gram_total[pl.ds(rank, rank), :]
    coupled = gram_total[pl.ds(2 * rank, patients), :]
    mats[0] = feature_gram * weight_gram + MU_RIDGE * identity
    mats[1] = core_gram * weight_gram + MU_RIDGE * identity
    mats[2] = core_gram * feature_gram + static_gram + MU_RIDGE * identity
    mats[3] = weight_gram + MU_RIDGE * identity
    inverses[...] = mats[...]

    lane_row = lax.broadcasted_iota(jnp.int32, (1, rank), 1)
    sub_col = lax.broadcasted_iota(jnp.int32, (rank, 1), 0)

    def eliminate(k):
        for m in range(4):
            whole = inverses[m]
            row = inverses[m, pl.ds(k, 1), :]
            pivot = jnp.sum(jnp.where(lane_row == k, row, 0.0), axis=1, keepdims=True)
            column = jnp.sum(jnp.where(lane == k, whole, 0.0), axis=1, keepdims=True)
            inverse = 1.0 / pivot
            scaled = jnp.where(lane_row == k, inverse, row * inverse)
            cleared = jnp.where((lane == k) | (sub == k), 0.0, whole)
            inverses[m] = cleared - jnp.where(sub_col == k, -1.0, column) * scaled

    share = rank // chunks

    def eliminate_some(c):
        @pl.loop(0, share)
        def _(j):
            eliminate(c * share + j)

    @pl.loop(lag, chunks)
    def _(c):
        relay(c)
        spread(c - lag)
        eliminate_some(c - lag)

    @pl.loop(chunks, chunks + lag)
    def _(c):
        spread(c - lag)
        eliminate_some(c - lag)

    blocks = rows // BLK
    group = 8
    starts, ends, lives = [], [], []
    position = jnp.int32(0)
    for k in range(patients):
        starts.append(position)
        lives.append(position + counts[k])
        position = position + ((counts[k] + (BLK - 1)) & (-BLK))
        ends.append(position)

    def coefficient(b, k):
        at = b * BLK
        return jnp.where((at >= starts[k]) & (at < ends[k]), 1.0, 0.0).astype(F32)

    start_row = jnp.full((1, rank), rows, jnp.int32)
    live_row = jnp.zeros((1, rank), jnp.int32)
    patient_col = lax.broadcasted_iota(jnp.int32, (patients, 1), 0)
    start_col = jnp.full((patients, 1), rows, jnp.int32)
    end_col = jnp.zeros((patients, 1), jnp.int32)
    for k in range(patients):
        start_row = jnp.where(lane_row == k, starts[k], start_row)
        live_row = jnp.where(lane_row == k, lives[k], live_row)
        start_col = jnp.where(patient_col == k, starts[k], start_col)
        end_col = jnp.where(patient_col == k, ends[k], end_col)
    weight_hi, weight_lo = split(
        jnp.concatenate([weight[...], jnp.zeros((rank - patients, rank), F32)], axis=0)
    )
    group_rows = group * BLK
    group_row = lax.broadcasted_iota(jnp.int32, (group_rows, rank), 0)

    def group_span(g):
        return pl.ds(pl.multiple_of(g * group_rows, group_rows), group_rows)

    @pl.loop(0, blocks // group)
    def _(g):
        at = group_row + g * group_rows
        live = jnp.where((at >= start_row) & (at < live_row), 1.0, 0.0).astype(BF16)
        by_row = dg(live, weight_hi, NN) + dg(live, weight_lo, NN)
        wide = total[group_span(g), :] * by_row
        row_weights[group_span(g), :] = by_row
        wides[group_span(g), :] = wide
        for i in range(group):
            one = wide[i * BLK : (i + 1) * BLK]
            squares[g * group + i] = dot3(one, one, TN)

    for k in range(patients):

        def add_blocks(g, acc, k=k):
            for i in range(group):
                b = g * group + i
                acc = acc + coefficient(b, k) * squares[b]
            return acc

        square = lax.fori_loop(0, blocks // group, add_blocks, jnp.zeros((rank, rank), F32))
        half = dot3(core[...], square)
        halves[k] = half
        gram = dot3(half, core[...], NT)
        trace = jnp.sum(jnp.sum(gram * identity, axis=1, keepdims=True), axis=0, keepdims=True)
        grams[k] = gram / trace
        factors[k] = identity / jnp.sqrt(trace)

    @pl.loop(0, NS_STEPS)
    def _(step):
        for k in range(patients):
            moment = grams[k]
            correction = 1.5 * identity - 0.5 * moment
            both = dot3(jnp.concatenate([factors[k], moment], axis=0), correction)
            factors[k] = both[:rank]
            grams[k] = dot3(correction, both[rank:])

    core_terms = jnp.zeros((rank, rank), F32)
    for k in range(patients):
        factor = factors[k]
        core_terms = core_terms + dot3(factor, halves[k], TN)
        grams[k] = dot3(core[...], dot3(factor, core[...]), TN)

    def core_copy(d):
        peer = lax.rem(me + d, n_pat)
        return remote(
            core_out.at[lax.rem(peer, owners)], core_in.at[me], core_send.at[d],
            core_recv.at[me], pat=peer,
        )

    core_out[...] = core_terms.reshape(owners, core_rows, rank)
    core_in[me] = core_out[lax.rem(me, owners)]
    for d in range(1, n_pat):
        core_copy(d).start()

    def map_group(g, sums):
        for i in range(group):
            b = g * group + i
            span_b = pl.ds(pl.multiple_of(b * BLK, BLK), BLK)
            mapper = coefficient(b, 0) * grams[0]
            for k in range(1, patients):
                mapper = mapper + coefficient(b, k) * grams[k]
            mapped = dot3(wides[span_b, :], mapper)
            products = mapped * total[span_b, :]
            updates[span_b, :] = (mapped * row_weights[span_b, :]).astype(BF16)
            at = b * BLK
            member = jnp.where((at >= start_col) & (at < end_col), 1.0, 0.0).astype(F32)
            sums = sums + member * jnp.sum(products, axis=0, keepdims=True)
        return sums

    patient_terms = lax.fori_loop(
        0, blocks // group, map_group, jnp.zeros((patients, rank), F32)
    )

    width = features // tiles
    per = n_pat // tiles

    def terms_copy(peer):
        return remote(
            terms_out.at[peer], terms_in.at[me], terms_send.at[peer], terms_recv.at[me], pat=peer
        )

    @pl.loop(0, tiles)
    def _(s):
        tile = lax.rem(lax.div(me, per) + 1 + s, tiles)
        columns = pl.ds(pl.multiple_of(tile * width, width), width)
        acc = jnp.zeros((width, rank), F32)
        for g in range(blocks // group):
            acc = acc + dg(
                vis[g * group_rows : (g + 1) * group_rows, columns],
                updates[g * group_rows : (g + 1) * group_rows, :],
                TN,
            )
        acc = solve(acc, mats[1], inverses[1]).astype(BF16)
        for j in range(per):
            peer = tile * per + j
            terms_out[peer] = acc[j * piece : (j + 1) * piece]

            @pl.when(peer != me)
            def _():
                terms_copy(peer).start()

    def each_peer(fn):
        for d in range(1, n_pat):
            fn(d, lax.rem(me + d, n_pat))

    def arrived(buffer, send, recv):
        def one(d, peer):
            remote(
                buffer.at[peer], buffer.at[peer], send.at[d], recv.at[peer], pat=peer
            ).wait_recv()

        each_peer(one)

    arrived(core_in, core_send, core_recv)
    terms_in[me] = terms_out[me]
    arrived(terms_in, terms_send, terms_recv)

    core_sum = jnp.sum(core_in[...], axis=0)
    coreg_out[...] = solve(core_sum, mats[0], inverses[0])
    terms_sum = jnp.sum(terms_in[...].astype(F32), axis=0)
    new_out[...] = terms_sum.astype(BF16)

    def new_copy(d):
        peer = lax.rem(me + d, n_pat)
        return remote(new_out, new_in.at[me], new_send.at[d], new_recv.at[me], pat=peer)

    def coreg_copy(d):
        peer = lax.rem(me + d, n_pat)
        return remote(coreg_out, coreg_in.at[me], coreg_send.at[d], coreg_recv.at[me], pat=peer)

    for d in range(1, n_pat):
        new_copy(d).start()
        coreg_copy(d).start()
    new_in[me] = new_out[...]
    coreg_in[me] = coreg_out[...]

    patient_new[...] = solve(
        patient_terms + coupled, mats[2], inverses[2]
    )
    static_terms = dot3(static_all[...].reshape(n_pat * patients, -1), all_rows, TN)
    static_new[...] = solve(static_terms, mats[3], inverses[3])

    arrived(coreg_in, coreg_send, coreg_recv)
    for q in range(owners):
        core_new[pl.ds(q * core_rows, core_rows), :] = coreg_in[q]
    arrived(new_in, new_send, new_recv)
    feature_new[...] = new_in[...].astype(F32).reshape(features, rank)

    for d in range(1, n_pat):
        weight_copy(d).wait_send()
        static_copy(d).wait_send()
        core_copy(d).wait_send()
        new_copy(d).wait_send()
        coreg_copy(d).wait_send()
        terms_copy(lax.rem(me + d, n_pat)).wait_send()

    @pl.when(z < gram_owner)
    def _():
        gram_part(True).wait_send()

        @pl.when(inner)
        def _():
            gram_back(False).wait_send()

    @pl.when(z > gram_owner)
    def _():
        gram_part(False).wait_send()

        @pl.when(outer)
        def _():
            gram_back(True).wait_send()

    @pl.when(z == gram_owner)
    def _():
        gram_back(False).wait_send()
        gram_back(True).wait_send()

    @pl.loop(0, chunks)
    def _(c):
        owner = owner_of(c)

        @pl.when(z < owner)
        def _():
            part_copy(c, True).wait_send()

            @pl.when(inner)
            def _():
                total_copy(c, False).wait_send()

        @pl.when(z > owner)
        def _():
            part_copy(c, False).wait_send()

            @pl.when(outer)
            def _():
                total_copy(c, True).wait_send()

        @pl.when(z == owner)
        def _():
            total_copy(c, False).wait_send()
            total_copy(c, True).wait_send()


def local(n_pat, n_feat, visits, counts, weight, core, factor, static_data, static_factor):
    rows, features = visits.shape
    patients, rank = weight.shape
    columns = static_data.shape[1]
    chunks = 16
    tiles = min(n_pat, features // 128)
    core_rows = max(rank // n_pat, 16)
    owners = rank // core_rows
    gram_rows = 2 * rank + patients
    piece = features // n_pat
    vmem, dma = pltpu.VMEM, pltpu.SemaphoreType.DMA
    scratch = [
        vmem((rows, features), BF16),
        vmem((rows, rank), F32),
        vmem((rows, rank), F32),
        vmem((rows, rank), F32),
        vmem((rows, rank), F32),
        vmem((rows, rank), F32),
        vmem((gram_rows, rank), F32),
        vmem((gram_rows, rank), F32),
        vmem((gram_rows, rank), F32),
        vmem((gram_rows, rank), F32),
        vmem((n_pat, patients, rank), F32),
        vmem((n_pat, patients, columns), F32),
        vmem((4, rank, rank), F32),
        vmem((4, rank, rank), F32),
        vmem((rows, rank), F32),
        vmem((rows, rank), F32),
        vmem((rows // BLK, rank, rank), F32),
        vmem((patients, rank, rank), F32),
        vmem((patients, rank, rank), F32),
        vmem((patients, rank, rank), F32),
        vmem((rows, rank), BF16),
        vmem((n_pat, piece, rank), BF16),
        vmem((n_pat, piece, rank), BF16),
        vmem((owners, core_rows, rank), F32),
        vmem((n_pat, core_rows, rank), F32),
        vmem((piece, rank), BF16),
        vmem((n_pat, piece, rank), BF16),
        vmem((core_rows, rank), F32),
        vmem((n_pat, core_rows, rank), F32),
        dma((chunks,)),
        dma((chunks,)),
        dma((chunks,)),
        dma((chunks,)),
        dma((2, chunks)),
        dma((chunks,)),
        dma((6,)),
    ] + [dma((n_pat,))] * 12
    space = pl.BlockSpec(memory_space=pltpu.VMEM)
    return pl.pallas_call(
        functools.partial(kernel, n_pat, n_feat, chunks, tiles),
        out_shape=(
            jax.ShapeDtypeStruct((rank, rank), F32),
            jax.ShapeDtypeStruct((features, rank), F32),
            jax.ShapeDtypeStruct((patients, rank), F32),
            jax.ShapeDtypeStruct((columns, rank), F32),
        ),
        in_specs=[
            pl.BlockSpec(memory_space=pltpu.SMEM),
            pl.BlockSpec(memory_space=pl.ANY),
            space, space, space, space, space,
        ],
        out_specs=(space, space, space, space),
        scratch_shapes=scratch,
        compiler_params=pltpu.CompilerParams(
            collective_id=0, has_side_effects=True, vmem_limit_bytes=62 * 1024 * 1024
        ),
        name="sweep",
    )(counts, visits, weight, core, factor, static_data, static_factor)


def solution(mesh):
    return jax.shard_map(
        functools.partial(local, mesh.shape["pat"], mesh.shape["feat"]),
        mesh=mesh,
        in_specs=(
            P("pat", "feat"),
            P("pat"),
            P("pat", None),
            P(),
            P("feat", None),
            P("pat", "feat"),
            P("feat", None),
        ),
        out_specs=(P(), P("feat", None), P("pat", None), P("feat", None)),
        check_vma=False,
    )
```

time: 357 us -> 207 us (0.58)
  Pallas kernels: 0 us -> 198 us
  waiting for transfers between devices: 136 us -> 0 us
  other arithmetic: 95.6 us -> 0 us
  matrix products: 94.2 us -> 0 us
  between operations: 14.9 us -> 0.64 us
  blocking collectives: 10.1 us -> 0 us
  local copies, waits for them, and re-layouts: 1.99 us -> 6.88 us
    pallas_call x0 -> x1, Pallas kernels: none -> 198 us  [local(): pl.pallas_call(functools.partial(kernel, n_pat, n_feat, chunks, tiles), o...]
    psum x2 -> x0, waiting for transfers between devices: 136 us -> none  [the longest x1 90.3 us: local(): lax.psum((projected_part, coupled_part, feature_gram_part, static_gram_pa...]
    another operation x23 -> x0, other arithmetic: 92.2 us -> none  [the longest x13 50.1 us: solve_right(): lower = jnp.linalg.cholesky(matrix)]
    dot_general x39 -> x0, matrix products: 84.6 us -> none  [the longest x22 15.5 us: batched(): jnp.einsum('nij,njk->nik', left, right, precision=lax.Precision.HIGHEST)]
    psum x1 -> x0, blocking collectives: 10.1 us -> none  [local(): lax.psum((projected_part, coupled_part, feature_gram_part, static_gram_pa...]
    another operation x8 -> x0, matrix products: 9.63 us -> none  [solve_right(): return jax.scipy.linalg.cho_solve((lower, True), rhs.T).T]
    unnamed x30 -> x4, local copies, waits for them, and re-layouts: 1.06 us -> 6.88 us
  transfers between devices with their start and end apart: 2 -> 0, of which waited for: 2 -> 0; matrix products, arithmetic and copies ran while one was open for 1% -> 0% of each run, Pallas kernels for 0% -> 0%
where the time goes in v1:
time: 207 us; the launch traced here: 206 us
  Pallas kernels  198 us (96%)
  local copies, waits for them, and re-layouts  6.88 us (3%)
    pallas_call x1, Pallas kernels, local(): pl.pallas_call(functools.partial(kernel, n_pat, n_feat, chunks, tiles), o...  198 us
    unnamed x4, local copies, waits for them, and re-layouts  6.88 us

profile of v1, /device:TPU:0, one launch (start us, length us, event | category | flops | bytes accessed | tf_op | source)
XLA Modules:
  0.0 205.8 jit_solution(6176669539019469982)
XLA Ops:
  0.6 198.3 %sweep.1 = (f32[128,128]{1,0:T(8,128)}, f32[2048,128]{1,0:T(8,128)}, f32[8,128]{1,0:T(8,128)}, f32[1024,128]{1,0:T(8,128)}) custom-call(s32[8]{0:T(128)} %counts.1, bf16[4096,2048]{1,0:T(8,128)(2,1)} %visits.1, f32[8,128]{1,0:T(8,128)} %weight.1, f32[128,128]{1,0:T(8,128)} %core.1, bf16[2048,128]{1,0:T(8,128)(2,1)} %factor_in.1, ...), custom_call_target="tpu_custom_call" | custom-call | tf_op jit(solution)/shard_map/sweep/pallas_call | solution.py:619
  198.9 1.5 copy.15
  200.4 2.3 %copy.16 = f32[2048,128]{1,0:T(8,128)} copy(f32[2048,128]{1,0:T(8,128)} %get-tuple-element.9) | data formatting | bytes 2097152
  202.7 1.3 copy.17
  203.9 1.9 copy.18
